TPU v7x, 32 devices: a whole 2x2x4 slice. The times are simulated.
32 devices in a mesh: dp: 8 (over y, x, core), tensor: 4 (over z).
Axes of the slice: x: 2, y: 2, z: 4, core: 2. Of those that a mesh axis runs over, the one named last changes fastest.
Arguments:
- hidden: bfloat16 [8192, 1536], P('dp'), may hold values from -6 to 6
- norm_gain: float32 [1536], replicated, may hold values from 0.25 to 1.75
- zx_proj: bfloat16 [1536, 2, 3072], P(None, None, 'tensor'), may hold values from -0.15625 to 0.15625
- bc_proj: bfloat16 [1536, 256], replicated, may hold values from -0.15625 to 0.15625
- dt_proj: bfloat16 [1536, 48], P(None, 'tensor'), may hold values from -0.15625 to 0.15625
- conv_x: float32 [5, 3072], P(None, 'tensor'), may hold values from -3 to 3
- conv_bc: float32 [5, 256], replicated, may hold values from -3 to 3
- dt_bias: float32 [48], P('tensor'), may hold values from -7 to -3
- a_log: float32 [48], P('tensor'), may hold values from -4 to 0.5
- d_skip: float32 [48], P('tensor'), may hold values from 0.5 to 1.5
- gate_gain: float32 [3072], P('tensor'), may hold values from 0.25 to 1.75
- out_proj: bfloat16 [1536, 3072], P(None, 'tensor'), may hold values from -0.109375 to 0.109375
- cotangent: bfloat16 [8192, 1536], P('dp'), may hold values from -6 to 6
Outputs:
- block_out: bfloat16 [8192, 1536], P('dp')
- grad_hidden: bfloat16 [8192, 1536], P('dp')
- grad_norm_gain: float32 [1536], replicated
- grad_zx_proj: float32 [1536, 2, 3072], P('dp', None, 'tensor')
- grad_bc_proj: float32 [1536, 256], P('dp')
- grad_dt_proj: float32 [1536, 48], P('dp', 'tensor')
- grad_conv_x: float32 [5, 3072], P(None, 'tensor')
- grad_conv_bc: float32 [5, 256], replicated
- grad_dt_bias: float32 [48], P('tensor')
- grad_a_log: float32 [48], P('tensor')
- grad_d_skip: float32 [48], P('tensor')
- grad_gate_gain: float32 [3072], P('tensor')
- grad_out_proj: float32 [1536, 3072], P('dp', 'tensor')
All inputs are finite; a program needn't handle non-finite values.
Results may differ from a plain program's by a relative error of at most 0.005.
The roundings to bfloat16 on the way count: a program that leaves them out, or rounds other values in their place, can miss the bound.
Values may be sent and summed in bfloat16 or wider, within the bound.
No kernel may reach another device: no remote copies, remote signals or barrier semaphores. Data moves between devices by JAX's collectives and lax.ppermute only.
A program may use at most 192 MiB of HBM per device.

v0:
```python
import jax
import jax.numpy as jnp
from jax import lax
from jax.sharding import PartitionSpec as P

KCONV = 4
BLOCK_LEN = 256
SEQ_DEVS = 8
EPSILON = 1e-05
PRECISE = lax.Precision.HIGHEST


def shifted(x, axis, by):
    length = lax.axis_size(axis)
    pairs = [(i, i + by) for i in range(length) if 0 <= i + by < length]
    return lax.ppermute(x, axis, pairs)


def swish_value(operand):
    return operand * jax.nn.sigmoid(operand)


def swish_slope(operand):
    logistic = jax.nn.sigmoid(operand)
    return logistic * (1.0 + operand * (1.0 - logistic))


def product_nt(first_op, second_op):
    return lax.dot_general(
        first_op, second_op, (((1,), (1,)), ((), ())), preferred_element_type=jnp.float32
    )


def product_tn(first_op, second_op):
    return lax.dot_general(
        first_op, second_op, (((0,), (0,)), ((), ())), preferred_element_type=jnp.float32
    )


def shards(
    hidden,
    norm_gain,
    zx_proj,
    bc_proj,
    dt_proj,
    conv_x,
    conv_bc,
    dt_bias,
    a_log,
    d_skip,
    gate_gain,
    out_proj,
    cotangent,
):
    tokens = hidden.shape[0]
    model_width = hidden.shape[1]
    inner_local = zx_proj.shape[2]
    heads_local = dt_proj.shape[1]
    head_size = inner_local // heads_local
    state_size = bc_proj.shape[1] // 2
    inner_total = inner_local * lax.axis_size("tensor")
    blocks = tokens // BLOCK_LEN
    position = lax.axis_index("dp") % SEQ_DEVS
    opens_seq = position == 0
    closes_seq = position == SEQ_DEVS - 1
    residual = hidden.astype(jnp.float32)
    inv_rms = lax.rsqrt(jnp.mean(residual * residual, axis=1, keepdims=True) + EPSILON)
    normed = residual * inv_rms
    normed_low = (normed * norm_gain).astype(jnp.bfloat16)
    zx_flat = zx_proj.reshape(model_width, 2 * inner_local)
    zx_out = jnp.dot(normed_low, zx_flat, preferred_element_type=jnp.float32)
    gate_low = zx_out[:, :inner_local].astype(jnp.bfloat16)
    bc_out = jnp.dot(normed_low, bc_proj, preferred_element_type=jnp.float32)
    dt_raw = jnp.dot(normed_low, dt_proj, preferred_element_type=jnp.float32)
    conv_in = jnp.concatenate(
        [zx_out[:, inner_local:].astype(jnp.bfloat16), bc_out.astype(jnp.bfloat16)], axis=1
    )
    conv_weights = jnp.concatenate([conv_x, conv_bc], axis=1)
    rim_rows = shifted(conv_in[tokens - (KCONV - 1) :], "dp", 1)
    rim_rows = jnp.where(opens_seq, jnp.zeros_like(rim_rows), rim_rows)
    padded = jnp.concatenate([rim_rows, conv_in], axis=0).astype(jnp.float32)
    conv_pre = conv_weights[KCONV] + conv_weights[0] * padded[0:tokens]
    for tap_index in range(1, KCONV):
        conv_pre = conv_pre + conv_weights[tap_index] * padded[tap_index : tap_index + tokens]
    conv_act = swish_value(conv_pre)
    inputs = conv_act[:, :inner_local].reshape(blocks, BLOCK_LEN, heads_local, head_size)
    b_rows = conv_act[:, inner_local : inner_local + state_size].reshape(
        blocks, BLOCK_LEN, state_size
    )
    c_rows = conv_act[:, inner_local + state_size :].reshape(blocks, BLOCK_LEN, state_size)
    dt_pre = dt_raw + dt_bias
    step_size = jax.nn.softplus(dt_pre)
    decay_rate = -jnp.exp(a_log)
    step_blocks = step_size.reshape(blocks, BLOCK_LEN, heads_local)
    cumulative = jnp.cumsum(
        (decay_rate * step_size).reshape(blocks, BLOCK_LEN, heads_local), axis=1
    )
    cumul_heads = jnp.swapaxes(cumulative, 1, 2)
    step_heads = jnp.swapaxes(step_blocks, 1, 2)
    row_index = lax.broadcasted_iota(jnp.int32, (BLOCK_LEN, BLOCK_LEN), 0)
    col_index = lax.broadcasted_iota(jnp.int32, (BLOCK_LEN, BLOCK_LEN), 1)
    within = (row_index >= col_index)[None, None, :, :]
    spread = cumul_heads[:, :, :, None] - cumul_heads[:, :, None, :]
    decay_pairs = jnp.where(within, jnp.exp(jnp.where(within, spread, 0.0)), 0.0)
    affinity = jnp.einsum("kin,kjn->kij", c_rows, b_rows, precision=PRECISE)
    pair_weight = decay_pairs * step_heads[:, :, None, :]
    mixing = affinity[:, None, :, :] * pair_weight
    intra_out = jnp.einsum("khij,kjhp->kihp", mixing, inputs, precision=PRECISE)
    end_exp = jnp.exp(cumulative[:, -1:, :] - cumulative)
    to_end = end_exp * step_blocks
    sent_state = jnp.einsum("kjhp,kjn->khpn", to_end[..., None] * inputs, b_rows, precision=PRECISE)
    block_decay = jnp.exp(cumulative[:, -1, :])
    zero_state = jnp.zeros((heads_local, head_size, state_size), jnp.float32)
    local_in = [zero_state]
    decay_before = [jnp.ones((heads_local,), jnp.float32)]
    for block_index in range(blocks):
        local_in.append(
            block_decay[block_index][:, None, None] * local_in[-1] + sent_state[block_index]
        )
        decay_before.append(decay_before[-1] * block_decay[block_index])
    own_state = local_in[blocks]
    own_decay = decay_before[blocks]
    entry_decay = jnp.where(opens_seq, 0.0, own_decay)

    def relay_state(turn_index, incoming):
        return shifted(entry_decay[:, None, None] * incoming + own_state, "dp", 1)

    arrived = lax.fori_loop(0, SEQ_DEVS - 1, relay_state, jnp.zeros_like(own_state))
    arrived = jnp.where(opens_seq, 0.0, arrived)
    states_in = (
        jnp.stack(local_in[:blocks]) + jnp.stack(decay_before[:blocks])[:, :, None, None] * arrived
    )
    exp_cumul = jnp.exp(cumulative)
    inter_out = exp_cumul[..., None] * jnp.einsum(
        "kin,khpn->kihp", c_rows, states_in, precision=PRECISE
    )
    ssd_out = intra_out + inter_out + d_skip[:, None] * inputs
    ssd_flat = ssd_out.reshape(tokens, inner_local)
    gate_wide = gate_low.astype(jnp.float32)
    gate_act = swish_value(gate_wide)
    gated_out = ssd_flat * gate_act
    gated_low = (gated_out * gate_gain).astype(jnp.bfloat16)
    partial_proj = product_nt(gated_low, out_proj)
    proj_sum, square_sum = lax.psum(
        (partial_proj, jnp.sum(gated_out * gated_out, axis=1)), "tensor"
    )
    inv_gate = lax.rsqrt(square_sum / inner_total + EPSILON)[:, None]
    block_out = (residual + inv_gate * proj_sum).astype(jnp.bfloat16)
    grad_top = cotangent.astype(jnp.float32)
    grad_proj = (inv_gate * grad_top).astype(jnp.bfloat16)
    grad_inv = jnp.sum(grad_top * proj_sum, axis=1, keepdims=True)
    grad_gated_low = jnp.dot(grad_proj, out_proj, preferred_element_type=jnp.float32)
    grad_out_local = product_tn(grad_proj, gated_low)
    grad_gate_gain = jnp.sum(grad_gated_low * gated_out, axis=0)
    grad_gated = (
        grad_gated_low * gate_gain
        - grad_inv * inv_gate * inv_gate * inv_gate / inner_total * gated_out
    )
    grad_ssd = (grad_gated * gate_act).reshape(blocks, BLOCK_LEN, heads_local, head_size)
    grad_gate = (grad_gated * ssd_flat * swish_slope(gate_wide)).astype(jnp.bfloat16)
    grad_skip = jnp.sum(grad_ssd * inputs, axis=(0, 1, 3))
    grad_scaled = grad_ssd * exp_cumul[..., None]
    grad_c = jnp.einsum("kihp,khpn->kin", grad_scaled, states_in, precision=PRECISE)
    grad_from_out = jnp.einsum("kihp,kin->khpn", grad_scaled, c_rows, precision=PRECISE)
    grad_cumul = jnp.sum(grad_ssd * inter_out, axis=3)
    grad_mixing = jnp.einsum("kihp,kjhp->khij", grad_ssd, inputs, precision=PRECISE)
    grad_inputs = d_skip[:, None] * grad_ssd + jnp.einsum(
        "khij,kihp->kjhp", mixing, grad_ssd, precision=PRECISE
    )
    grad_affinity = jnp.sum(grad_mixing * pair_weight, axis=1)
    grad_pairs = grad_mixing * affinity[:, None, :, :] * decay_pairs
    grad_step = jnp.swapaxes(jnp.sum(grad_pairs, axis=2), 1, 2)
    grad_spread = grad_pairs * step_heads[:, :, None, :]
    grad_cumul = grad_cumul + jnp.swapaxes(
        jnp.sum(grad_spread, axis=3) - jnp.sum(grad_spread, axis=2), 1, 2
    )
    grad_c = grad_c + jnp.einsum("kij,kjn->kin", grad_affinity, b_rows, precision=PRECISE)
    grad_b = jnp.einsum("kij,kin->kjn", grad_affinity, c_rows, precision=PRECISE)
    local_grad = [zero_state]
    decay_after = [jnp.ones((heads_local,), jnp.float32)]
    for block_index in reversed(range(blocks)):
        local_grad.insert(
            0, grad_from_out[block_index] + block_decay[block_index][:, None, None] * local_grad[0]
        )
        decay_after.insert(0, decay_after[0] * block_decay[block_index])
    own_grad = local_grad[0]
    exit_decay = jnp.where(closes_seq, 0.0, own_decay)

    def relay_grad(turn_index, incoming):
        return shifted(exit_decay[:, None, None] * incoming + own_grad, "dp", -1)

    back_arrived = lax.fori_loop(0, SEQ_DEVS - 1, relay_grad, jnp.zeros_like(own_grad))
    back_arrived = jnp.where(closes_seq, 0.0, back_arrived)
    grad_states = jnp.stack(local_grad) + jnp.stack(decay_after)[:, :, None, None] * back_arrived
    grad_send = grad_states[1:]
    state_back = jnp.einsum("khpn,kjn->kjhp", grad_send, b_rows, precision=PRECISE)
    grad_to_end = jnp.sum(inputs * state_back, axis=3)
    grad_inputs = grad_inputs + to_end[..., None] * state_back
    grad_b = grad_b + jnp.einsum(
        "kjhp,khpn->kjn", to_end[..., None] * inputs, grad_send, precision=PRECISE
    )
    grad_step = grad_step + grad_to_end * end_exp
    weighted = grad_to_end * to_end
    grad_last = jnp.sum(weighted, axis=1) + block_decay * jnp.sum(
        grad_send * states_in, axis=(2, 3)
    )
    grad_cumul = (grad_cumul - weighted).at[:, -1, :].add(grad_last)
    grad_log = jnp.flip(jnp.cumsum(jnp.flip(grad_cumul, 1), axis=1), 1).reshape(tokens, heads_local)
    grad_a_log = decay_rate * jnp.sum(grad_log * step_size, axis=0)
    grad_dt_pre = (grad_step.reshape(tokens, heads_local) + decay_rate * grad_log) * jax.nn.sigmoid(
        dt_pre
    )
    grad_dt_bias = jnp.sum(grad_dt_pre, axis=0)
    grad_dt_low = grad_dt_pre.astype(jnp.bfloat16)
    grad_bc_act = lax.psum(
        jnp.concatenate([grad_b, grad_c], axis=2).reshape(tokens, 2 * state_size), "tensor"
    )
    grad_act = jnp.concatenate([grad_inputs.reshape(tokens, inner_local), grad_bc_act], axis=1)
    grad_pre = grad_act * swish_slope(conv_pre)
    rim_back = shifted(grad_pre[: KCONV - 1], "dp", -1)
    rim_back = jnp.where(closes_seq, 0.0, rim_back)
    extended = jnp.concatenate([grad_pre, rim_back], axis=0)
    grad_conv_in = conv_weights[0] * extended[KCONV - 1 : KCONV - 1 + tokens]
    for tap_index in range(1, KCONV):
        grad_conv_in = (
            grad_conv_in
            + conv_weights[tap_index]
            * extended[KCONV - 1 - tap_index : KCONV - 1 - tap_index + tokens]
        )
    grad_taps = jnp.stack(
        [
            jnp.sum(grad_pre * padded[tap_index : tap_index + tokens], axis=0)
            for tap_index in range(KCONV)
        ]
        + [jnp.sum(grad_pre, axis=0)]
    )
    grad_inner_low = grad_conv_in[:, :inner_local].astype(jnp.bfloat16)
    grad_bc_low = grad_conv_in[:, inner_local:].astype(jnp.bfloat16)
    grad_zx_low = jnp.concatenate([grad_gate, grad_inner_low], axis=1)
    grad_normed_part = product_nt(grad_zx_low, zx_flat) + product_nt(grad_dt_low, dt_proj)
    grad_normed = lax.psum(grad_normed_part, "tensor") + product_nt(grad_bc_low, bc_proj)
    grad_norm_local = jnp.sum(grad_normed * normed, axis=0)
    grad_scaled_in = grad_normed * norm_gain
    grad_resid = inv_rms * (
        grad_scaled_in - normed * jnp.mean(grad_scaled_in * normed, axis=1, keepdims=True)
    )
    grad_hidden = (grad_top + grad_resid).astype(jnp.bfloat16)
    grad_zx_local = product_tn(normed_low, grad_zx_low).reshape(model_width, 2, inner_local)
    grad_bc_local = product_tn(normed_low, grad_bc_low)
    grad_dt_local = product_tn(normed_low, grad_dt_low)
    grad_zx_proj, grad_bc_proj, grad_dt_proj, grad_out_proj = (
        lax.psum_scatter(grad_zx_local, "dp", scatter_dimension=0, tiled=True),
        lax.psum_scatter(grad_bc_local, "dp", scatter_dimension=0, tiled=True),
        lax.psum_scatter(grad_dt_local, "dp", scatter_dimension=0, tiled=True),
        lax.psum_scatter(grad_out_local, "dp", scatter_dimension=0, tiled=True),
    )
    (
        grad_norm_gain,
        grad_conv_x,
        grad_conv_bc,
        grad_dt_bias,
        grad_a_log,
        grad_d_skip,
        grad_gate_gain,
    ) = lax.psum(
        (
            grad_norm_local,
            grad_taps[:, :inner_local],
            grad_taps[:, inner_local:],
            grad_dt_bias,
            grad_a_log,
            grad_skip,
            grad_gate_gain,
        ),
        "dp",
    )
    return (
        block_out,
        grad_hidden,
        grad_norm_gain,
        grad_zx_proj,
        grad_bc_proj,
        grad_dt_proj,
        grad_conv_x,
        grad_conv_bc,
        grad_dt_bias,
        grad_a_log,
        grad_d_skip,
        grad_gate_gain,
        grad_out_proj,
    )


def solution(mesh):
    in_specs = (
        P("dp", None),
        P(),
        P(None, None, "tensor"),
        P(),
        P(None, "tensor"),
        P(None, "tensor"),
        P(),
        P("tensor"),
        P("tensor"),
        P("tensor"),
        P("tensor"),
        P(None, "tensor"),
        P("dp", None),
    )
    out_specs = (
        P("dp", None),
        P("dp", None),
        P(),
        P("dp", None, "tensor"),
        P("dp", None),
        P("dp", "tensor"),
        P(None, "tensor"),
        P(),
        P("tensor"),
        P("tensor"),
        P("tensor"),
        P("tensor"),
        P("dp", "tensor"),
    )
    return jax.shard_map(shards, mesh=mesh, in_specs=in_specs, out_specs=out_specs, check_vma=False)
```

profile of v0, /device:TPU:0, one launch (start us, length us, event | category | flops | bytes accessed | tf_op | source)
XLA Modules:
  0.0 1144.8 jit_solution(1173458592556442112)
XLA Ops:
  69.6 59.2 %while.21 = (s32[]{:T(128)}, f32[12,64,128]{2,1,0:T(8,128)S(1)}, f32[12]{0:T(128)S(1)}, f32[12,64,128]{2,1,0:T(8,128)S(1)}, s32[]{:T(128)}) while((s32[]{:T(128)}, f32[12,64,128]{2,1,0:T(8,128)S(1)}, f32[12]{0:T(128)S(1)}, f32[12,64,128]{2,1,0:T(8,128)S(1)}, s32[]{:T(128)}) %tuple.107), condition=%wide.region_4.5_spmd, body=%wide.region_3.4_spmd.sunk | while | flops 196610 | bytes 2752661 | solution.py:128
  82.6 7.8 collective-permute-start
  91.8 7.8 collective-permute-start
  134.9 15.0 %fusion.50 = f32[4,256,12,64]{1,3,2,0:T(8,128)S(1)} fusion(f32[4,256,12,64]{1,3,2,0:T(8,128)S(1)} %fusion.134, f32[4,256,12,64]{1,0,3,2:T(4,128)S(1)} %copy-done.4, f32[4,12,256]{2,1,0:T(8,128)S(1)} %copy-done.59, f32[4,12,256]{2,1,0:T(8,128)S(1)} %copy-done.58, f32[4,256,256]{2,1,0:T(8,128)S(1)} %fusion.141, pred[256,256]{1,0:T(8,128)(4,1)S(1)} %copy-done.61, ...), kind=kOutput, calls=%fused_computation.80 | convolution fusion | flops 2434793472 | bytes 10698800 | tf_op jit(solution)/shard_map/khij,kjhp->kihp/dot_general | solution.py:108
  168.5 12.0 %psum.77 = f32[1024]{0:T(1024)S(1)} all-reduce(f32[1024]{0:T(1024)S(1)} %get-tuple-element.116), channel_id=1, replica_groups=mesh['dp'=8,'tensor'=4] {'tensor'}, use_global_device_ids=true, to_apply=%region_6.7 | all-reduce | flops 1024 | bytes 8192 | tf_op jit(solution)/shard_map/psum | solution.py:144
  180.6 223.6 %all-reduce.7.cloned.1.call-done = f32[1024,1536]{1,0:T(8,128)} async-done(((f32[1024,1536]{1,0:T(8,128)}), f32[1024,1536]{1,0:T(8,128)}) %all-reduce.7.cloned.1.call-update) | async-done | bytes 6291472 | tf_op jit(solution)/shard_map/psum | solution.py:144
  436.7 65.4 %while.22 = (s32[]{:T(128)}, f32[12,64,128]{2,1,0:T(8,128)S(1)}, f32[12]{0:T(128)S(1)}, f32[12,64,128]{2,1,0:T(8,128)S(1)}, s32[]{:T(128)}) while((s32[]{:T(128)}, f32[12,64,128]{2,1,0:T(8,128)S(1)}, f32[12]{0:T(128)S(1)}, f32[12,64,128]{2,1,0:T(8,128)S(1)}, s32[]{:T(128)}) %tuple.106), condition=%wide.region_10.11_spmd, body=%wide.region_9.10_spmd.sunk | while | flops 196610 | bytes 2752661 | solution.py:192
  453.1 8.0 collective-permute-done.1
  463.2 8.0 collective-permute-done.1
  473.4 8.0 collective-permute-done.1
  483.5 8.0 collective-permute-done.1
  493.7 8.0 collective-permute-done.1
  515.9 20.0 %multiply_reduce_fusion.1 = (f32[4,12,256]{2,1,0:T(8,128)}, f32[4,12,256]{2,1,0:T(8,128)}, f32[4,12,256]{2,1,0:T(8,128)}, f32[4,256,256]{2,1,0:T(8,128)S(1)}) fusion(f32[4,12,256]{2,1,0:T(8,128)S(1)} %copy-done.59, f32[4,12,256]{2,1,0:T(8,128)S(1)} %copy-done.58, pred[256,256]{1,0:T(8,128)(4,1)S(1)} %copy-done.62, f32[4,256,256]{2,1,0:T(8,128)S(1)} %copy-done.48, ...), kind=kOutput, calls=%fused_computation.9 | convolution fusion | flops 2453368832 | bytes 8699904 | tf_op jit(solution)/shard_map/kihp,kjhp->khij/dot_general | solution.py:166
  540.5 12.9 %fusion.49 = f32[4,256,12,64]{1,3,2,0:T(8,128)} fusion(f32[4,256,12,64]{1,3,2,0:T(8,128)S(1)} %get-tuple-element.158, f32[4,256,12,64]{1,0,3,2:T(4,128)S(1)} %copy-done.9, f32[4,12,256]{2,1,0:T(8,128)S(1)} %copy-done.60, f32[4,12,256]{2,1,0:T(8,128)S(1)} %copy-done.58, f32[4,256,256]{2,1,0:T(8,128)S(1)} %copy-done.48, pred[256,256]{1,0:T(8,128)(4,1)S(1)} %copy-done.62, ...), kind=kOutput, calls=%fused_computation.78 | convolution fusion | flops 2434793472 | bytes 10698800 | tf_op jit(solution)/shard_map/khij,kihp->kjhp/dot_general | solution.py:167
  586.2 35.3 %all-reduce.9.cloned.1.call-done = f32[1024,256]{1,0:T(8,128)} async-done(((f32[1024,256]{1,0:T(8,128)}), f32[1024,256]{1,0:T(8,128)}) %all-reduce.9.cloned.1.call-update) | async-done | bytes 1048592 | tf_op jit(solution)/shard_map/psum | solution.py:215
  621.6 10.5 multiply_reduce_fusion.3
  655.3 15.0 %copy.307 = f32[1536,2,768]{2,1,0:T(2,128)} copy(f32[1536,2,768]{0,2,1:T(8,128)} %bitcast.208) | data formatting | bytes 18874368 | tf_op jit(solution)/shard_map/reshape | solution.py:248
  670.3 7.9 fusion.70
  682.9 7.9 fusion.83
  698.9 114.5 %all-reduce.13.cloned.1.call-done = f32[1536,2,768]{2,1,0:T(2,128)} async-done(((f32[1536,2,768]{2,1,0:T(2,128)}), f32[1536,2,768]{2,1,0:T(2,128)}) %all-reduce.13.cloned.1.call-update) | async-done | bytes 9437200
  816.1 222.5 %all-reduce.11.cloned.1.call-done = f32[1024,1536]{1,0:T(8,128)} async-done(((f32[1024,1536]{1,0:T(8,128)}), f32[1024,1536]{1,0:T(8,128)}) %all-reduce.11.cloned.1.call-update) | async-done | bytes 6291472 | tf_op jit(solution)/shard_map/psum | solution.py:241
  1045.1 25.4 %all-reduce.1 = (f32[1536]{0:T(1024)}, f32[5,768]{1,0:T(8,128)}, f32[5,256]{1,0:T(8,128)}, f32[12]{0:T(128)}, f32[12]{0:T(128)}, /*index=5*/f32[12]{0:T(128)}, f32[768]{0:T(1024)}) all-reduce(f32[1536]{0:T(1024)S(1)} %get-tuple-element.75, f32[5,768]{1,0:T(8,128)S(1)} %slice.249, ...), channel_id=1, replica_groups=mesh['dp'=8,'tensor'=4] {'dp'}, use_global_device_ids=true, to_apply=%region_25.26 | all-reduce | flops 7460 | bytes 59680 | tf_op jit(solution)/shard_map/psum | solution.py:265
  1077.5 17.7 %reduce-scatter.8.cloned.1.call-done = f32[192,768]{1,0:T(8,128)} async-done(((f32[1536,768]{1,0:T(8,128)}), f32[192,768]{1,0:T(8,128)}) %reduce-scatter.8.cloned.1.call-update) | async-done | bytes 589840 | tf_op jit(solution)/shard_map/reduce_scatter | solution.py:255
  1095.2 42.2 %reduce-scatter.6.cloned.1.call-done = f32[192,256]{1,0:T(8,128)} async-done(((f32[1536,256]{1,0:T(8,128)}), f32[192,256]{1,0:T(8,128)}) %reduce-scatter.6.cloned.1.call-update) | async-done | bytes 196624 | tf_op jit(solution)/shard_map/reduce_scatter | solution.py:253
  (398 shorter events, 289.0 us)
Async XLA Ops:
  7.2 397.0 %all-reduce.7.cloned.1.call-start = ((), (), s32[]{:S(2)}) async-start(), calls=%async_computation.3 | async-start | bytes 12582912 | tf_op jit(solution)/shard_map/psum | solution.py:144
  24.5 19.6 %collective-permute-start.2 = (bf16[3,1024]{1,0:T(4,128)(2,1)S(1)}, bf16[3,1024]{1,0:T(4,128)(2,1)}, u32[]{:S(2)}, u32[]{:S(2)}) collective-permute-start(bf16[3,1024]{1,0:T(4,128)(2,1)S(1)} %pad_maximum_fusion.5), channel_id=1, source_target_pairs={{0,4},{4,8},{8,12},{12,16},{16,20},{20,24},{24,28},{1,5},{5,9},{9,... | collective-permute-start | bytes 18440 | tf_op jit(solution)/shard_map/ppermute | solution.py:16
  69.8 6.0 collective-permute-start
  75.8 6.6 collective-permute-start
  82.6 9.1 collective-permute-start
  91.8 9.1 collective-permute-start
  101.0 9.1 collective-permute-start
  110.2 9.1 collective-permute-start
  119.4 9.1 collective-permute-start
  167.8 453.7 %all-reduce.9.cloned.1.call-start = ((), (), s32[]{:S(2)}) async-start(), calls=%async_computation.4 | async-start | bytes 2097152 | tf_op jit(solution)/shard_map/psum | solution.py:215
  437.6 3.8 collective-permute-start.1
  442.3 8.6 collective-permute-start.1
  451.8 9.3 collective-permute-start.1
  461.9 9.3 collective-permute-start.1
  472.1 9.3 collective-permute-start.1
  482.2 9.3 collective-permute-start.1
  492.4 9.3 collective-permute-start.1
  559.6 137.6 %reduce-scatter.10.cloned.1.call-start = ((), (), s32[]{:S(2)}) async-start(), calls=%async_computation.8 | async-start | bytes 884736
  634.0 3.6 collective-permute-start.3
  637.3 176.1 %all-reduce.13.cloned.1.call-start = ((), (), s32[]{:S(2)}) async-start(), calls=%async_computation.9 | async-start | bytes 18874368
  670.3 368.3 %all-reduce.11.cloned.1.call-start = ((), (), s32[]{:S(2)}) async-start(), calls=%async_computation.5 | async-start | bytes 12582912 | tf_op jit(solution)/shard_map/psum | solution.py:241
  682.3 412.9 %reduce-scatter.8.cloned.1.call-start = ((), (), s32[]{:S(2)}) async-start(), calls=%async_computation.7 | async-start | bytes 5308416 | tf_op jit(solution)/shard_map/reduce_scatter | solution.py:255
  690.9 446.5 %reduce-scatter.6.cloned.1.call-start = ((), (), s32[]{:S(2)}) async-start(), calls=%async_computation.6 | async-start | bytes 1769472 | tf_op jit(solution)/shard_map/reduce_scatter | solution.py:253
  697.1 341.5 %copy-start.64 = (f32[1024]{0:T(1024)S(1)}, f32[1024]{0:T(1024)}, u32[]{:S(2)}) copy-start(f32[1024]{0:T(1024)} %copy-done.63) | copy-start | bytes 12292
  (104 other events, 1934.7 us)
Sparse Core Ops, SparseCore 0:
  168.0 236.1 all-reduce.6
  559.7 61.8 all-reduce.8
  637.4 34.9 reduce-scatter.9
  675.7 137.6 all-reduce.12
  815.6 222.9 all-reduce.10
  1042.4 52.7 reduce-scatter.7
  1099.1 38.3 reduce-scatter.5
where the time goes:
time: 1150 us; the launch traced here: 1140 us
  waiting for transfers between devices  715 us (62%)
  matrix products  139 us (12%)
  local copies, waits for them, and re-layouts  97 us (8%)
  other arithmetic  75.5 us (7%)
  starting transfers between devices  63.3 us (6%)
  blocking collectives  37.4 us (3%)
  between operations  16.7 us (1%)
    psum x1, waiting for transfers between devices, shards(): lax.psum((partial_proj, jnp.sum(gated_out * gated_out, axis=1)), 'tensor')  224 us
    psum x1, waiting for transfers between devices, shards(): lax.psum(grad_normed_part, 'tensor') + product_nt(grad_bc_low, bc_proj)  222 us
    unnamed x9, waiting for transfers between devices  115 us
    ppermute x16, starting transfers between devices, shifted(): return lax.ppermute(x, axis, pairs)  62.3 us
    ppermute x16, waiting for transfers between devices, shifted(): return lax.ppermute(x, axis, pairs)  59 us
    reduce_scatter x1, waiting for transfers between devices, shards(): lax.psum_scatter(grad_bc_local, 'dp', scatter_dimension=0, tiled=True)  42.2 us
    psum x1, waiting for transfers between devices, shards(): lax.psum(jnp.concatenate([grad_b, grad_c], axis=2).reshape(tokens, 2 * st...  35.3 us
    unnamed x222, local copies, waits for them, and re-layouts  32 us
  transfers between devices with their start and end apart: 23, of which 20 were waited for; matrix products, arithmetic and copies ran while one was open for 10% of the time, Pallas kernels for 0%

commit v1 on v0

--- a/solution.py
+++ b/solution.py
@@ -212,8 +212,11 @@
     )
     grad_dt_bias = jnp.sum(grad_dt_pre, axis=0)
     grad_dt_low = grad_dt_pre.astype(jnp.bfloat16)
-    grad_bc_act = lax.psum(
-        jnp.concatenate([grad_b, grad_c], axis=2).reshape(tokens, 2 * state_size), "tensor"
+    grad_bc_act = jnp.sum(
+        lax.all_gather(
+            jnp.concatenate([grad_b, grad_c], axis=2).reshape(tokens, 2 * state_size), "tensor"
+        ),
+        axis=0,
     )
     grad_act = jnp.concatenate([grad_inputs.reshape(tokens, inner_local), grad_bc_act], axis=1)
     grad_pre = grad_act * swish_slope(conv_pre)

time: 1150 us -> 1160 us (level)
    all_gather x0 -> x1, waiting for transfers between devices: none -> 43.1 us  [shards(): lax.all_gather(jnp.concatenate([grad_b, grad_c], axis=2).reshape(tokens,...]
    psum x1 -> x0, waiting for transfers between devices: 35.3 us -> none  [shards(): lax.psum(jnp.concatenate([grad_b, grad_c], axis=2).reshape(tokens, 2 * st...]
    unnamed x222 -> x244, local copies, waits for them, and re-layouts: 32 us -> 31.2 us
  transfers between devices with their start and end apart: 23 -> 23, of which waited for: 20 -> 20; matrix products, arithmetic and copies ran while one was open for 10% -> 12% of each run, Pallas kernels for 0% -> 0%
where the time goes in v1:
time: 1160 us
  waiting for transfers between devices  721 us (62%)
  matrix products  142 us (12%)
  local copies, waits for them, and re-layouts  97.5 us (8%)
  other arithmetic  77.7 us (7%)
  starting transfers between devices  63.5 us (5%)
  blocking collectives  37.3 us (3%)
  between operations  16.6 us (1%)
    psum x1, waiting for transfers between devices, shards(): lax.psum((partial_proj, jnp.sum(gated_out * gated_out, axis=1)), 'tensor')  224 us
    psum x1, waiting for transfers between devices, shards(): lax.psum(grad_normed_part, 'tensor') + product_nt(grad_bc_low, bc_proj)  222 us
    unnamed x9, waiting for transfers between devices  114 us
    ppermute x16, starting transfers between devices, shifted(): return lax.ppermute(x, axis, pairs)  62.8 us
    ppermute x16, waiting for transfers between devices, shifted(): return lax.ppermute(x, axis, pairs)  57.6 us
    all_gather x1, waiting for transfers between devices, shards(): lax.all_gather(jnp.concatenate([grad_b, grad_c], axis=2).reshape(tokens,...  43.1 us
    reduce_scatter x1, waiting for transfers between devices, shards(): lax.psum_scatter(grad_bc_local, 'dp', scatter_dimension=0, tiled=True)  42.2 us
    unnamed x244, local copies, waits for them, and re-layouts  31.2 us
  transfers between devices with their start and end apart: 23, of which 20 were waited for; matrix products, arithmetic and copies ran while one was open for 12% of the time, Pallas kernels for 0%

profile of v1, /device:TPU:0, one launch (start us, length us, event | category | flops | bytes accessed | tf_op | source)
XLA Modules:
  0.0 1156.7 jit_solution(5371803938681601307)
XLA Ops:
  69.8 59.3 %while.21 = (s32[]{:T(128)}, f32[12,64,128]{2,1,0:T(8,128)S(1)}, f32[12]{0:T(128)S(1)}, f32[12,64,128]{2,1,0:T(8,128)S(1)}, s32[]{:T(128)}) while((s32[]{:T(128)}, f32[12,64,128]{2,1,0:T(8,128)S(1)}, f32[12]{0:T(128)S(1)}, f32[12,64,128]{2,1,0:T(8,128)S(1)}, s32[]{:T(128)}) %tuple.106), condition=%wide.region_4.5_spmd, body=%wide.region_3.4_spmd.sunk | while | flops 196610 | bytes 2752661 | solution.py:128
  91.9 7.8 collective-permute-start
  110.3 7.8 collective-permute-start
  134.5 15.0 %fusion.50 = f32[4,256,12,64]{1,3,2,0:T(8,128)S(1)} fusion(f32[4,256,12,64]{1,3,2,0:T(8,128)S(1)} %fusion.134, f32[4,256,12,64]{1,0,3,2:T(4,128)S(1)} %copy-done.4, f32[4,12,256]{2,1,0:T(8,128)S(1)} %copy-done.71, f32[4,12,256]{2,1,0:T(8,128)S(1)} %copy-done.68, f32[4,256,256]{2,1,0:T(8,128)S(1)} %fusion.141, pred[256,256]{1,0:T(8,128)(4,1)S(1)} %copy-done.74, ...), kind=kOutput, calls=%fused_computation.80 | convolution fusion | flops 2434793472 | bytes 10698800 | tf_op jit(solution)/shard_map/khij,kjhp->kihp/dot_general | solution.py:108
  168.0 12.0 %psum.70 = f32[1024]{0:T(1024)S(1)} all-reduce(f32[1024]{0:T(1024)S(1)} %get-tuple-element.116), channel_id=1, replica_groups=mesh['dp'=8,'tensor'=4] {'tensor'}, use_global_device_ids=true, to_apply=%region_6.7 | all-reduce | flops 1024 | bytes 8192 | tf_op jit(solution)/shard_map/psum | solution.py:144
  180.0 223.6 %all-reduce.6.cloned.1.call-done = f32[1024,1536]{1,0:T(8,128)} async-done(((f32[1024,1536]{1,0:T(8,128)}), f32[1024,1536]{1,0:T(8,128)}) %all-reduce.6.cloned.1.call-update) | async-done | bytes 6291472 | tf_op jit(solution)/shard_map/psum | solution.py:144
  437.5 20.6 %multiply_reduce_fusion.1 = (f32[4,12,256]{2,1,0:T(8,128)}, f32[4,12,256]{2,1,0:T(8,128)}, f32[4,12,256]{2,1,0:T(8,128)}, f32[4,256,256]{2,1,0:T(8,128)}) fusion(f32[4,12,256]{2,1,0:T(8,128)S(1)} %copy-done.72, f32[4,12,256]{2,1,0:T(8,128)S(1)} %copy-done.69, pred[256,256]{1,0:T(8,128)(4,1)S(1)} %copy-done.75, f32[4,256,256]{2,1,0:T(8,128)S(1)} %copy-done.56, ...), kind=kOutput, calls=%fused_computation.9 | convolution fusion | flops 2453368832 | bytes 8699904 | tf_op jit(solution)/shard_map/kihp,kjhp->khij/dot_general | solution.py:166
  462.4 62.5 %while.22 = (s32[]{:T(128)}, f32[12,64,128]{2,1,0:T(8,128)S(1)}, f32[12]{0:T(128)}, f32[12,64,128]{2,1,0:T(8,128)S(1)}, s32[]{:T(128)}) while((s32[]{:T(128)}, f32[12,64,128]{2,1,0:T(8,128)S(1)}, f32[12]{0:T(128)}, f32[12,64,128]{2,1,0:T(8,128)S(1)}, s32[]{:T(128)}) %tuple.89), condition=%wide.region_10.11_spmd, body=%wide.region_9.10_spmd.sunk | while | flops 196610 | bytes 2752661 | solution.py:192
  477.9 7.8 collective-permute-done.1
  487.7 7.8 collective-permute-done.1
  497.5 7.8 collective-permute-done.1
  507.3 7.8 collective-permute-done.1
  517.1 7.8 collective-permute-done.1
  547.0 12.2 %fusion.49 = f32[4,256,12,64]{1,3,2,0:T(8,128)S(1)} fusion(f32[4,256,12,64]{1,3,2,0:T(8,128)S(1)} %get-tuple-element.158, f32[4,256,12,64]{1,0,3,2:T(4,128)S(1)} %copy-done.11, f32[4,12,256]{2,1,0:T(8,128)S(1)} %copy-done.73, f32[4,12,256]{2,1,0:T(8,128)S(1)} %copy-done.70, f32[4,256,256]{2,1,0:T(8,128)S(1)} %copy-done.57, ...), kind=kOutput, calls=%fused_computation.78 | convolution fusion | flops 2434793472 | bytes 10698800 | tf_op jit(solution)/shard_map/khij,kihp->kjhp/dot_general | solution.py:167
  588.4 43.1 %all-gather.2.cloned.1.call-done = f32[4,1024,256]{2,1,0:T(8,128)} async-done(((f32[1,1024,256]{2,1,0:T(8,128)}), f32[4,1024,256]{2,1,0:T(8,128)}) %all-gather.2.cloned.1.call-update) | async-done | bytes 4194320 | tf_op jit(solution)/shard_map/all_gather | solution.py:216
  634.2 10.5 multiply_reduce_fusion.3
  667.9 14.8 %copy.306 = f32[1536,2,768]{2,1,0:T(2,128)} copy(f32[1536,2,768]{0,2,1:T(8,128)} %bitcast.208) | data formatting | bytes 18874368 | tf_op jit(solution)/shard_map/reshape | solution.py:251
  682.8 7.9 fusion.70
  695.4 7.9 fusion.83
  711.4 114.3 %all-reduce.10.cloned.1.call-done = f32[1536,2,768]{2,1,0:T(2,128)} async-done(((f32[1536,2,768]{2,1,0:T(2,128)}), f32[1536,2,768]{2,1,0:T(2,128)}) %all-reduce.10.cloned.1.call-update) | async-done | bytes 9437200
  828.3 222.5 %all-reduce.8.cloned.1.call-done = f32[1024,1536]{1,0:T(8,128)} async-done(((f32[1024,1536]{1,0:T(8,128)}), f32[1024,1536]{1,0:T(8,128)}) %all-reduce.8.cloned.1.call-update) | async-done | bytes 6291472 | tf_op jit(solution)/shard_map/psum | solution.py:244
  1057.3 25.3 %all-reduce.1 = (f32[1536]{0:T(1024)}, f32[5,768]{1,0:T(8,128)}, f32[5,256]{1,0:T(8,128)}, f32[12]{0:T(128)}, f32[12]{0:T(128)}, /*index=5*/f32[12]{0:T(128)}, f32[768]{0:T(1024)}) all-reduce(f32[1536]{0:T(1024)S(1)} %get-tuple-element.75, f32[5,768]{1,0:T(8,128)S(1)} %slice.249, ...), channel_id=1, replica_groups=mesh['dp'=8,'tensor'=4] {'dp'}, use_global_device_ids=true, to_apply=%region_25.26 | all-reduce | flops 7460 | bytes 59680 | tf_op jit(solution)/shard_map/psum | solution.py:268
  1089.7 17.8 %reduce-scatter.8.cloned.1.call-done = f32[192,768]{1,0:T(8,128)} async-done(((f32[1536,768]{1,0:T(8,128)}), f32[192,768]{1,0:T(8,128)}) %reduce-scatter.8.cloned.1.call-update) | async-done | bytes 589840 | tf_op jit(solution)/shard_map/reduce_scatter | solution.py:258
  1107.5 42.2 %reduce-scatter.6.cloned.1.call-done = f32[192,256]{1,0:T(8,128)} async-done(((f32[1536,256]{1,0:T(8,128)}), f32[192,256]{1,0:T(8,128)}) %reduce-scatter.6.cloned.1.call-update) | async-done | bytes 196624 | tf_op jit(solution)/shard_map/reduce_scatter | solution.py:256
  (421 shorter events, 295.0 us)
Async XLA Ops:
  7.2 396.4 %all-reduce.6.cloned.1.call-start = ((), (), s32[]{:S(2)}) async-start(), calls=%async_computation.3 | async-start | bytes 12582912 | tf_op jit(solution)/shard_map/psum | solution.py:144
  24.5 19.6 %collective-permute-start.2 = (bf16[3,1024]{1,0:T(4,128)(2,1)S(1)}, bf16[3,1024]{1,0:T(4,128)(2,1)}, u32[]{:S(2)}, u32[]{:S(2)}) collective-permute-start(bf16[3,1024]{1,0:T(4,128)(2,1)S(1)} %pad_maximum_fusion.5), channel_id=1, source_target_pairs={{0,4},{4,8},{8,12},{12,16},{16,20},{20,24},{24,28},{1,5},{5,9},{9,... | collective-permute-start | bytes 18440 | tf_op jit(solution)/shard_map/ppermute | solution.py:16
  69.9 6.0 collective-permute-start
  76.0 6.6 collective-permute-start
  82.7 9.1 collective-permute-start
  91.9 9.1 collective-permute-start
  101.1 9.1 collective-permute-start
  110.3 9.1 collective-permute-start
  119.5 9.1 collective-permute-start
  167.3 464.3 %all-gather.2.cloned.1.call-start = ((), (), s32[]{:S(2)}) async-start(), calls=%async_computation.4 | async-start | bytes 5242880 | tf_op jit(solution)/shard_map/all_gather | solution.py:216
  463.1 3.6 collective-permute-start.1
  467.4 8.5 collective-permute-start.1
  476.6 9.1 collective-permute-start.1
  486.4 9.1 collective-permute-start.1
  496.2 9.1 collective-permute-start.1
  506.0 9.1 collective-permute-start.1
  515.8 9.1 collective-permute-start.1
  540.8 168.9 %reduce-scatter.10.cloned.1.call-start = ((), (), s32[]{:S(2)}) async-start(), calls=%async_computation.8 | async-start | bytes 884736
  646.7 3.7 collective-permute-start.3
  650.3 175.3 %all-reduce.10.cloned.1.call-start = ((), (), s32[]{:S(2)}) async-start(), calls=%async_computation.9 | async-start | bytes 18874368
  682.8 368.1 %all-reduce.8.cloned.1.call-start = ((), (), s32[]{:S(2)}) async-start(), calls=%async_computation.5 | async-start | bytes 12582912 | tf_op jit(solution)/shard_map/psum | solution.py:244
  694.8 412.7 %reduce-scatter.8.cloned.1.call-start = ((), (), s32[]{:S(2)}) async-start(), calls=%async_computation.7 | async-start | bytes 5308416 | tf_op jit(solution)/shard_map/reduce_scatter | solution.py:258
  703.4 446.3 %reduce-scatter.6.cloned.1.call-start = ((), (), s32[]{:S(2)}) async-start(), calls=%async_computation.6 | async-start | bytes 1769472 | tf_op jit(solution)/shard_map/reduce_scatter | solution.py:256
  709.6 341.3 %copy-start.78 = (f32[1024]{0:T(1024)S(1)}, f32[1024]{0:T(1024)}, u32[]{:S(2)}) copy-start(f32[1024]{0:T(1024)} %copy-done.77) | copy-start | bytes 12292
  (115 other events, 2070.7 us)
Sparse Core Ops, SparseCore 0:
  167.4 236.1 all-reduce.5
  540.8 90.6 all-gather.1
  650.5 34.1 reduce-scatter.9
  688.0 137.6 all-reduce.9
  827.9 222.9 all-reduce.7
  1054.7 52.7 reduce-scatter.7
  1111.3 38.3 reduce-scatter.5
